TPU v7x, 32 devices: a whole 2x2x4 slice. The times are simulated.
32 devices in a mesh: src: 4 (over z), delay: 8 (over y, x, core).
Axes of the slice: x: 2, y: 2, z: 4, core: 2. Of those that a mesh axis runs over, the one named last changes fastest.
Arguments:
- history: float32 [32, 16, 16, 128], P('delay', 'src'), may hold values from -6 to 6
- slot_map: int32 [32], P('delay'), may hold values from 0 to 3, as said below
- interaction: float32 [1536, 128, 128], P(('src', 'delay')), may hold values from -0.0546875 to 0.0546875
- pattern: int32 [3, 1536], P(None, ('src', 'delay')), may hold values from 0 to 15, as said below
- live: int32 [32], P(('src', 'delay')), may hold values from 12 to 48
- near_inverse: float32 [16, 128, 128], P('src'), may hold values from -0.5 to 0.5
- incident: float32 [4, 16, 16, 128], P(None, 'src'), may hold values from -6 to 6
Outputs:
- currents: float32 [4, 16, 16, 128], P(None, 'src')
Inputs may be any that keep to these rules, and one draw needn't show every extreme that they name: `slot_map`: each band's 4 entries are a cyclic rotation of 0 .. 3. `pattern`: row 0 lies in 0 .. 3, row 1 in 0 .. 15, row 2 in 0 .. 3.
All inputs are finite; a program needn't handle non-finite values.
Results may differ from a plain program's by a relative error of at most 0.0003.
Values sent between devices are 32-bit elements; how exact they have to be, the bound alone decides.
No kernel may reach another device: no remote copies, remote signals or barrier semaphores. Data moves between devices by JAX's collectives and lax.ppermute only.
A program may use at most 64 MiB of HBM per device.

v0:
```python
import jax
import jax.numpy as jnp
from jax import lax
from jax.sharding import PartitionSpec as P


def shifted(x, axis, by):
    devices = lax.axis_size(axis)
    pairs = [(i, i + by) for i in range(devices) if 0 <= i + by < devices]
    return lax.ppermute(x, axis, pairs)


def slot_holding(slot_map, wanted, moment):
    length = slot_map.shape[0]
    positions = jnp.arange(length, dtype=jnp.int32)
    return jnp.sum(jnp.where((slot_map + moment) % length == wanted, positions, 0))


def body(history, slot_map, interaction, pattern, live, near_inverse, incident):
    slot_count = history.shape[0]
    group_blocks = history.shape[1]
    columns = history.shape[2]
    block_width = history.shape[3]
    moments = incident.shape[0]
    pair_count = interaction.shape[0]
    positions = jnp.arange(slot_count, dtype=jnp.int32)
    at_front = lax.axis_index("delay") == 0
    in_use = (jnp.arange(pair_count, dtype=jnp.int32) < live[0]).astype(jnp.float32)
    row_match = pattern[0][None, :] == jnp.arange(group_blocks, dtype=jnp.int32)[:, None]
    selector = row_match.astype(jnp.float32) * in_use[None, :]
    band_state = lax.all_gather(history, "src", axis=1, tiled=True)
    results = []
    newest = None
    for moment in range(moments):
        if moment > 0:
            vacated = slot_holding(slot_map, slot_count - 1, moment - 1)
            outgoing_slot = lax.dynamic_index_in_dim(band_state, vacated, 0, keepdims=False)
            incoming = shifted(outgoing_slot, "delay", 1)
            entering = jnp.where(at_front, newest, incoming)
            band_state = lax.dynamic_update_index_in_dim(band_state, entering, vacated, 0)
        holder_match = (slot_map[None, :] + moment) % slot_count == pattern[2][:, None]
        holder = jnp.sum(jnp.where(holder_match, positions[None, :], 0), axis=1)
        picked = band_state[holder, pattern[1]]
        products = jnp.einsum("pab,prb->pra", interaction, picked, precision=lax.Precision.HIGHEST)
        partial_field = jnp.dot(
            selector,
            products.reshape(pair_count, columns * block_width),
            precision=lax.Precision.HIGHEST,
        )
        partial_field = partial_field.reshape(group_blocks, columns, block_width)
        field_sum = lax.psum(partial_field, "delay")
        current = jnp.einsum(
            "iab,irb->ira",
            near_inverse,
            incident[moment] - field_sum,
            precision=lax.Precision.HIGHEST,
        )
        results.append(current)
        if moment + 1 < moments:
            newest = lax.all_gather(current, "src", axis=0, tiled=True)
    return jnp.stack(results)


def solution(mesh):
    return jax.shard_map(
        body,
        mesh=mesh,
        in_specs=(
            P("delay", "src", None, None),
            P("delay"),
            P(("src", "delay"), None, None),
            P(None, ("src", "delay")),
            P(("src", "delay")),
            P("src", None, None),
            P(None, "src", None, None),
        ),
        out_specs=P(None, "src", None, None),
        check_vma=False,
    )
```

profile of v0, /device:TPU:4, one launch (start us, length us, event | category | flops | bytes accessed | tf_op | source)
XLA Modules:
  0.0 216.7 jit_solution(3523601571943106550)
XLA Ops:
  0.0 1.5 fusion.45
  1.5 18.1 %all_gather.12 = f32[4,16,16,128]{3,2,1,0:T(8,128)} all-gather(f32[4,4,16,128]{3,2,1,0:T(8,128)} %param.7), channel_id=1, replica_groups=mesh['src'=4,'delay'=8] {'src'}, dimensions={1}, use_global_device_ids=true | all-gather | bytes 655360 | tf_op jit(solution)/shard_map/all_gather | solution.py:31
  21.5 1.6 dynamic-slice_bitcast_fusion.2
  23.1 1.9 collective-permute-start
  26.6 2.6 %gather_fusion = f32[48,16,128]{2,1,0:T(8,128)} fusion(f32[4,16,16,128]{3,2,1,0:T(8,128)} %all_gather.12, s32[48]{0:T(128)S(1)} %get-tuple-element.25), kind=kCustom, calls=%fused_computation | custom fusion | bytes 786816 | tf_op jit(solution)/shard_map/gather | solution.py:43
  29.9 6.0 %fusion.74 = f32[48,16,128]{2,1,0:T(8,128)S(1)} fusion(f32[48,16,128]{2,1,0:T(8,128)} %gather_fusion, f32[48,128,128]{2,1,0:T(8,128)S(1)} %copy-done), kind=kOutput, calls=%fused_computation.121 | convolution fusion | flops 150994944 | bytes 3932160 | tf_op jit(solution)/shard_map/pab,prb->pra/dot_general | solution.py:44
  36.3 24.8 %psum.28 = f32[4,16,128]{2,0,1:T(4,128)S(1)} all-reduce(f32[4,16,128]{2,0,1:T(4,128)S(1)} %fusion.9), channel_id=1, replica_groups=mesh['src'=4,'delay'=8] {'delay'}, use_global_device_ids=true, to_apply=%region_1.2 | all-reduce | flops 8192 | bytes 65536 | tf_op jit(solution)/shard_map/psum | solution.py:51
  61.1 1.4 fusion.73
  66.7 13.4 %all_gather.13 = f32[16,16,128]{2,1,0:T(8,128)S(1)} all-gather(f32[4,16,128]{2,1,0:T(8,128)S(1)} %fusion.21), channel_id=1, replica_groups=mesh['src'=4,'delay'=8] {'src'}, dimensions={0}, use_global_device_ids=true | all-gather | bytes 163840 | tf_op jit(solution)/shard_map/all_gather | solution.py:60
  80.0 1.6 bitcast_dynamic-update-slice_fusion.2
  81.6 2.6 %gather_fusion.1 = f32[48,16,128]{2,1,0:T(8,128)} fusion(f32[4,16,16,128]{3,2,1,0:T(8,128)} %bitcast_dynamic-update-slice_fusion.2, s32[48]{0:T(128)S(1)} %get-tuple-element.24), kind=kCustom, calls=%fused_computation.1 | custom fusion | bytes 786816 | tf_op jit(solution)/shard_map/gather | solution.py:43
  84.3 6.0 %fusion.75 = f32[48,16,128]{2,1,0:T(8,128)S(1)} fusion(f32[48,16,128]{2,1,0:T(8,128)} %gather_fusion.1, f32[48,128,128]{2,1,0:T(8,128)S(1)} %copy-done), kind=kOutput, calls=%fused_computation.122 | convolution fusion | flops 150994944 | bytes 3932160 | tf_op jit(solution)/shard_map/pab,prb->pra/dot_general | solution.py:44
  90.2 1.0 fusion.6
  91.3 22.9 %psum.29 = f32[4,16,128]{2,0,1:T(4,128)S(1)} all-reduce(f32[4,16,128]{2,0,1:T(4,128)} %fusion.6), channel_id=1, replica_groups=mesh['src'=4,'delay'=8] {'delay'}, use_global_device_ids=true, to_apply=%region_4.5 | all-reduce | flops 8192 | bytes 65536 | tf_op jit(solution)/shard_map/psum | solution.py:51
  115.1 1.9 collective-permute-start.1
  117.6 13.9 %all_gather.14 = f32[16,16,128]{2,1,0:T(8,128)S(1)} all-gather(f32[4,16,128]{2,1,0:T(8,128)S(1)} %fusion.19), channel_id=1, replica_groups=mesh['src'=4,'delay'=8] {'src'}, dimensions={0}, use_global_device_ids=true | all-gather | bytes 163840 | tf_op jit(solution)/shard_map/all_gather | solution.py:60
  132.1 2.6 %gather_fusion.2 = f32[48,16,128]{2,1,0:T(8,128)} fusion(f32[4,16,16,128]{3,2,1,0:T(8,128)} %bitcast_dynamic-update-slice_fusion.1, s32[48]{0:T(128)S(1)} %get-tuple-element.23), kind=kCustom, calls=%fused_computation.2 | custom fusion | bytes 786816 | tf_op jit(solution)/shard_map/gather | solution.py:43
  134.7 6.0 %fusion.76 = f32[48,16,128]{2,1,0:T(8,128)S(1)} fusion(f32[48,16,128]{2,1,0:T(8,128)} %gather_fusion.2, f32[48,128,128]{2,1,0:T(8,128)S(1)} %copy-done), kind=kOutput, calls=%fused_computation.123 | convolution fusion | flops 150994944 | bytes 3932160 | tf_op jit(solution)/shard_map/pab,prb->pra/dot_general | solution.py:44
  141.7 22.9 %psum.30 = f32[4,16,128]{2,0,1:T(4,128)S(1)} all-reduce(f32[4,16,128]{2,0,1:T(4,128)} %fusion.3), channel_id=1, replica_groups=mesh['src'=4,'delay'=8] {'delay'}, use_global_device_ids=true, to_apply=%region_7.8 | all-reduce | flops 8192 | bytes 65536 | tf_op jit(solution)/shard_map/psum | solution.py:51
  165.6 1.9 collective-permute-start.2
  168.0 13.5 %all_gather.15 = f32[16,16,128]{2,1,0:T(8,128)S(1)} all-gather(f32[4,16,128]{2,1,0:T(8,128)S(1)} %fusion.17), channel_id=1, replica_groups=mesh['src'=4,'delay'=8] {'src'}, dimensions={0}, use_global_device_ids=true | all-gather | bytes 163840 | tf_op jit(solution)/shard_map/all_gather | solution.py:60
  182.2 2.6 %gather_fusion.3 = f32[48,16,128]{2,1,0:T(8,128)} fusion(f32[4,16,16,128]{3,2,1,0:T(8,128)} %bitcast_dynamic-update-slice_fusion, s32[48]{0:T(128)S(1)} %get-tuple-element.9), kind=kCustom, calls=%fused_computation.3 | custom fusion | bytes 786816 | tf_op jit(solution)/shard_map/gather | solution.py:43
  184.9 6.0 %fusion.77 = f32[48,16,128]{2,1,0:T(8,128)S(1)} fusion(f32[48,16,128]{2,1,0:T(8,128)} %gather_fusion.3, f32[48,128,128]{2,1,0:T(8,128)S(1)} %copy-done), kind=kOutput, calls=%fused_computation.124 | convolution fusion | flops 150994944 | bytes 3932160 | tf_op jit(solution)/shard_map/pab,prb->pra/dot_general | solution.py:44
  191.9 22.9 %psum.31 = f32[4,16,128]{2,0,1:T(4,128)S(1)} all-reduce(f32[4,16,128]{2,0,1:T(4,128)} %fusion), channel_id=1, replica_groups=mesh['src'=4,'delay'=8] {'delay'}, use_global_device_ids=true, to_apply=%region_10.11 | all-reduce | flops 8192 | bytes 65536 | tf_op jit(solution)/shard_map/psum | solution.py:51
  (34 shorter events, 10.8 us)
Async XLA Ops:
  0.0 29.9 %copy-start = (f32[48,128,128]{2,1,0:T(8,128)S(1)}, f32[48,128,128]{2,1,0:T(8,128)}, u32[]{:S(2)}) copy-start(f32[48,128,128]{2,1,0:T(8,128)} %param.9) | copy-start | bytes 9437188
  1.5 61.0 %copy-start.1 = (f32[4,128,128]{2,1,0:T(8,128)S(1)}, f32[4,128,128]{2,1,0:T(8,128)}, u32[]{:S(2)}) copy-start(f32[4,128,128]{2,1,0:T(8,128)} %param.12) | copy-start | bytes 786436
  23.1 56.9 %collective-permute-start = (f32[16,16,128]{2,1,0:T(8,128)}, f32[16,16,128]{2,1,0:T(8,128)}, u32[]{:S(2)}, u32[]{:S(2)}) collective-permute-start(f32[16,16,128]{2,1,0:T(8,128)} %dynamic-slice_bitcast_fusion.2), channel_id=1, source_target_pairs={{0,1},{1,2},{2,3},{3,4},{4,5},{5,6},{6,7},{8,9},{9,10},{10,11},{11... | collective-permute-start | bytes 393224 | tf_op jit(solution)/shard_map/ppermute | solution.py:10
  29.9 6.0 %copy-start.2 = (f32[48]{0:T(128)}, f32[48]{0:T(128)S(1)}, u32[]{:S(2)}) copy-start(f32[48]{0:T(128)S(1)} %compare_convert_fusion) | copy-start | bytes 580
  62.5 27.7 %copy-start.3 = (f32[48]{0:T(128)S(1)}, f32[48]{0:T(128)}, u32[]{:S(2)}) copy-start(f32[48]{0:T(128)} %copy-done.2) | copy-start | bytes 580
  90.2 50.5 %copy-start.4 = (f32[48]{0:T(128)S(1)}, f32[48]{0:T(128)}, u32[]{:S(2)}) copy-start(f32[48]{0:T(128)} %copy-done.2) | copy-start | bytes 580
  115.1 16.3 %collective-permute-start.1 = (f32[16,16,128]{2,1,0:T(8,128)S(1)}, f32[16,16,128]{2,1,0:T(8,128)S(1)}, u32[]{:S(2)}, u32[]{:S(2)}) collective-permute-start(f32[16,16,128]{2,1,0:T(8,128)S(1)} %dynamic-slice_bitcast_fusion.1), channel_id=1, source_target_pairs={{0,1},{1,2},{2,3},{3,4},{4,5},{5,6},{6,7},{8,9},{9,10},{10,11},{11... | collective-permute-start | bytes 393224 | tf_op jit(solution)/shard_map/ppermute | solution.py:10
  165.6 16.0 %collective-permute-start.2 = (f32[16,16,128]{2,1,0:T(8,128)S(1)}, f32[16,16,128]{2,1,0:T(8,128)S(1)}, u32[]{:S(2)}, u32[]{:S(2)}) collective-permute-start(f32[16,16,128]{2,1,0:T(8,128)S(1)} %dynamic-slice_bitcast_fusion), channel_id=1, source_target_pairs={{0,1},{1,2},{2,3},{3,4},{4,5},{5,6},{6,7},{8,9},{9,10},{10,11},{11... | collective-permute-start | bytes 393224 | tf_op jit(solution)/shard_map/ppermute | solution.py:10
where the time goes:
time: 218 us; the launch traced here: 217 us
  blocking collectives  152 us (70%)
  matrix products  29.4 us (13%)
  local copies, waits for them, and re-layouts  16.2 us (7%)
  other arithmetic  6.73 us (3%)
  between operations  6.34 us (3%)
  starting transfers between devices  5.75 us (3%)
    psum x4, blocking collectives, body(): field_sum = lax.psum(partial_field, 'delay')  93.5 us
    all_gather x3, blocking collectives, body(): newest = lax.all_gather(current, 'src', axis=0, tiled=True)  40.7 us
    dot_general x4, matrix products, body(): jnp.einsum('pab,prb->pra', interaction, picked, precision=lax.Precision.H...  23.8 us
    all_gather x1, blocking collectives, body(): band_state = lax.all_gather(history, 'src', axis=1, tiled=True)  18.1 us
    gather x4, local copies, waits for them, and re-layouts, body(): picked = band_state[holder, pattern[1]]  10.6 us
    ppermute x3, starting transfers between devices, shifted(): return lax.ppermute(x, axis, pairs)  5.75 us
  transfers between devices with their start and end apart: 3, of which 0 were waited for; matrix products, arithmetic and copies ran while one was open for 6% of the time, Pallas kernels for 0%

commit v1 on v0

--- a/solution.py
+++ b/solution.py
@@ -48,7 +48,7 @@
             precision=lax.Precision.HIGHEST,
         )
         partial_field = partial_field.reshape(group_blocks, columns, block_width)
-        field_sum = lax.psum(partial_field, "delay")
+        field_sum = jnp.sum(lax.all_gather(partial_field, "delay"), axis=0)
         current = jnp.einsum(
             "iab,irb->ira",
             near_inverse,

time: 218 us -> 171 us (0.78); the launches traced: 217 us -> 167 us
  blocking collectives: 152 us -> 97.9 us
  other arithmetic: 6.73 us -> 12.7 us
    psum x4 -> x0, blocking collectives: 93.5 us -> none  [body(): field_sum = lax.psum(partial_field, 'delay')]
    all_gather x0 -> x4, blocking collectives: none -> 39.5 us  [body(): field_sum = jnp.sum(lax.all_gather(partial_field, 'delay'), axis=0)]
    reduce_sum x0 -> x4, other arithmetic: none -> 3.89 us  [body(): field_sum = jnp.sum(lax.all_gather(partial_field, 'delay'), axis=0)]
  transfers between devices with their start and end apart: 3 -> 3, of which waited for: 0 -> 0; matrix products, arithmetic and copies ran while one was open for 6% -> 9% of each run, Pallas kernels for 0% -> 0%
where the time goes in v1:
time: 171 us; the launch traced here: 167 us
  blocking collectives  97.9 us (57%)
  matrix products  27.5 us (16%)
  local copies, waits for them, and re-layouts  16 us (9%)
  other arithmetic  12.7 us (7%)
  starting transfers between devices  6.56 us (4%)
  between operations  6.51 us (4%)
    all_gather x3, blocking collectives, body(): newest = lax.all_gather(current, 'src', axis=0, tiled=True)  40.3 us
    all_gather x4, blocking collectives, body(): field_sum = jnp.sum(lax.all_gather(partial_field, 'delay'), axis=0)  39.5 us
    dot_general x4, matrix products, body(): jnp.einsum('pab,prb->pra', interaction, picked, precision=lax.Precision.H...  23.8 us
    all_gather x1, blocking collectives, body(): band_state = lax.all_gather(history, 'src', axis=1, tiled=True)  18.1 us
    gather x4, local copies, waits for them, and re-layouts, body(): picked = band_state[holder, pattern[1]]  10.6 us
    ppermute x3, starting transfers between devices, shifted(): return lax.ppermute(x, axis, pairs)  6.56 us
    reduce_sum x4, other arithmetic, body(): field_sum = jnp.sum(lax.all_gather(partial_field, 'delay'), axis=0)  3.89 us
  transfers between devices with their start and end apart: 3, of which 0 were waited for; matrix products, arithmetic and copies ran while one was open for 9% of the time, Pallas kernels for 0%

profile of v1, /device:TPU:4, one launch (start us, length us, event | category | flops | bytes accessed | tf_op | source)
XLA Modules:
  0.0 167.2 jit_solution(2118773219303339827)
XLA Ops:
  0.0 2.1 %fusion.45 = (s32[]{:T(128)}, s32[4]{0:T(128)S(1)}, s32[]{:T(128)}, s32[4]{0:T(128)S(1)}, s32[]{:T(128)}, /*index=5*/s32[4]{0:T(128)}, s32[4]{0:T(128)}) fusion(s32[4]{0:T(128)} %param.8), kind=kLoop, calls=%fused_computation.91 | loop fusion | flops 221 | bytes 92 | tf_op jit(solution)/shard_map/reduce_sum | solution.py:16
  2.1 18.1 %all_gather.24 = f32[4,16,16,128]{3,2,1,0:T(8,128)} all-gather(f32[4,4,16,128]{3,2,1,0:T(8,128)} %param.7), channel_id=1, replica_groups=mesh['src'=4,'delay'=8] {'src'}, dimensions={1}, use_global_device_ids=true | all-gather | bytes 655360 | tf_op jit(solution)/shard_map/all_gather | solution.py:31
  22.1 1.6 dynamic-slice_bitcast_fusion.2
  23.7 2.0 %collective-permute-start = (f32[16,16,128]{2,1,0:T(8,128)}, f32[16,16,128]{2,1,0:T(8,128)}, u32[]{:S(2)}, u32[]{:S(2)}) collective-permute-start(f32[16,16,128]{2,1,0:T(8,128)} %dynamic-slice_bitcast_fusion.2), channel_id=1, source_target_pairs={{0,1},{1,2},{2,3},{3,4},{4,5},{5,6},{6,7},{8,9},{9,10},{10,11},{11... | collective-permute-start | bytes 393224 | tf_op jit(solution)/shard_map/ppermute | solution.py:10
  25.7 1.3 slice_bitcast_fusion.1
  28.5 2.6 %gather_fusion = f32[48,16,128]{2,1,0:T(8,128)} fusion(f32[4,16,16,128]{3,2,1,0:T(8,128)} %all_gather.24, s32[48]{0:T(128)S(1)} %get-tuple-element.25), kind=kCustom, calls=%fused_computation | custom fusion | bytes 786816 | tf_op jit(solution)/shard_map/gather | solution.py:43
  31.8 6.0 %fusion.74 = f32[48,16,128]{2,1,0:T(8,128)S(1)} fusion(f32[48,16,128]{2,1,0:T(8,128)} %gather_fusion, f32[48,128,128]{2,1,0:T(8,128)S(1)} %copy-done), kind=kOutput, calls=%fused_computation.121 | convolution fusion | flops 150994944 | bytes 3932160 | tf_op jit(solution)/shard_map/pab,prb->pra/dot_general | solution.py:44
  38.2 10.4 %all-gather = f32[32,16,128]{2,1,0:T(8,128)} all-gather(f32[4,16,128]{2,1,0:T(8,128)S(1)} %copy.34), channel_id=2, replica_groups=mesh['src'=4,'delay'=8] {'delay'}, dimensions={0}, use_global_device_ids=true | all-gather | bytes 294912 | tf_op jit(solution)/shard_map/all_gather | solution.py:51
  49.3 1.0 reduce_sum.109
  55.3 13.3 %all_gather.26 = f32[16,16,128]{2,1,0:T(8,128)S(1)} all-gather(f32[4,16,128]{2,1,0:T(8,128)S(1)} %fusion.21), channel_id=1, replica_groups=mesh['src'=4,'delay'=8] {'src'}, dimensions={0}, use_global_device_ids=true | all-gather | bytes 163840 | tf_op jit(solution)/shard_map/all_gather | solution.py:60
  68.7 1.6 bitcast_dynamic-update-slice_fusion.2
  70.3 2.6 %gather_fusion.1 = f32[48,16,128]{2,1,0:T(8,128)} fusion(f32[4,16,16,128]{3,2,1,0:T(8,128)} %bitcast_dynamic-update-slice_fusion.2, s32[48]{0:T(128)S(1)} %get-tuple-element.24), kind=kCustom, calls=%fused_computation.1 | custom fusion | bytes 786816 | tf_op jit(solution)/shard_map/gather | solution.py:43
  72.9 6.0 %fusion.75 = f32[48,16,128]{2,1,0:T(8,128)S(1)} fusion(f32[48,16,128]{2,1,0:T(8,128)} %gather_fusion.1, f32[48,128,128]{2,1,0:T(8,128)S(1)} %copy-done), kind=kOutput, calls=%fused_computation.122 | convolution fusion | flops 150994944 | bytes 3932160 | tf_op jit(solution)/shard_map/pab,prb->pra/dot_general | solution.py:44
  79.3 9.4 %all-gather.1 = f32[32,16,128]{2,1,0:T(8,128)} all-gather(f32[4,16,128]{2,1,0:T(8,128)S(1)} %copy.39), channel_id=3, replica_groups=mesh['src'=4,'delay'=8] {'delay'}, dimensions={0}, use_global_device_ids=true | all-gather | bytes 294912 | tf_op jit(solution)/shard_map/all_gather | solution.py:51
  90.6 2.3 %collective-permute-start.1 = (f32[16,16,128]{2,1,0:T(8,128)S(1)}, f32[16,16,128]{2,1,0:T(8,128)S(1)}, u32[]{:S(2)}, u32[]{:S(2)}) collective-permute-start(f32[16,16,128]{2,1,0:T(8,128)S(1)} %dynamic-slice_bitcast_fusion.1), channel_id=1, source_target_pairs={{0,1},{1,2},{2,3},{3,4},{4,5},{5,6},{6,7},{8,9},{9,10},{10,11},{11... | collective-permute-start | bytes 393224 | tf_op jit(solution)/shard_map/ppermute | solution.py:10
  93.4 13.6 %all_gather.28 = f32[16,16,128]{2,1,0:T(8,128)S(1)} all-gather(f32[4,16,128]{2,1,0:T(8,128)S(1)} %fusion.19), channel_id=1, replica_groups=mesh['src'=4,'delay'=8] {'src'}, dimensions={0}, use_global_device_ids=true | all-gather | bytes 163840 | tf_op jit(solution)/shard_map/all_gather | solution.py:60
  107.7 2.6 %gather_fusion.2 = f32[48,16,128]{2,1,0:T(8,128)} fusion(f32[4,16,16,128]{3,2,1,0:T(8,128)} %bitcast_dynamic-update-slice_fusion.1, s32[48]{0:T(128)S(1)} %get-tuple-element.23), kind=kCustom, calls=%fused_computation.2 | custom fusion | bytes 786816 | tf_op jit(solution)/shard_map/gather | solution.py:43
  110.3 6.0 %fusion.76 = f32[48,16,128]{2,1,0:T(8,128)S(1)} fusion(f32[48,16,128]{2,1,0:T(8,128)} %gather_fusion.2, f32[48,128,128]{2,1,0:T(8,128)S(1)} %copy-done), kind=kOutput, calls=%fused_computation.123 | convolution fusion | flops 150994944 | bytes 3932160 | tf_op jit(solution)/shard_map/pab,prb->pra/dot_general | solution.py:44
  116.7 10.2 %all-gather.2 = f32[32,16,128]{2,1,0:T(8,128)} all-gather(f32[4,16,128]{2,1,0:T(8,128)S(1)} %copy.44), channel_id=4, replica_groups=mesh['src'=4,'delay'=8] {'delay'}, dimensions={0}, use_global_device_ids=true | all-gather | bytes 294912 | tf_op jit(solution)/shard_map/all_gather | solution.py:51
  128.8 2.3 %collective-permute-start.2 = (f32[16,16,128]{2,1,0:T(8,128)S(1)}, f32[16,16,128]{2,1,0:T(8,128)S(1)}, u32[]{:S(2)}, u32[]{:S(2)}) collective-permute-start(f32[16,16,128]{2,1,0:T(8,128)S(1)} %dynamic-slice_bitcast_fusion), channel_id=1, source_target_pairs={{0,1},{1,2},{2,3},{3,4},{4,5},{5,6},{6,7},{8,9},{9,10},{10,11},{11... | collective-permute-start | bytes 393224 | tf_op jit(solution)/shard_map/ppermute | solution.py:10
  131.6 13.4 %all_gather.30 = f32[16,16,128]{2,1,0:T(8,128)S(1)} all-gather(f32[4,16,128]{2,1,0:T(8,128)S(1)} %fusion.17), channel_id=1, replica_groups=mesh['src'=4,'delay'=8] {'src'}, dimensions={0}, use_global_device_ids=true | all-gather | bytes 163840 | tf_op jit(solution)/shard_map/all_gather | solution.py:60
  145.7 2.6 %gather_fusion.3 = f32[48,16,128]{2,1,0:T(8,128)} fusion(f32[4,16,16,128]{3,2,1,0:T(8,128)} %bitcast_dynamic-update-slice_fusion, s32[48]{0:T(128)S(1)} %get-tuple-element.9), kind=kCustom, calls=%fused_computation.3 | custom fusion | bytes 786816 | tf_op jit(solution)/shard_map/gather | solution.py:43
  148.3 6.0 %fusion.77 = f32[48,16,128]{2,1,0:T(8,128)S(1)} fusion(f32[48,16,128]{2,1,0:T(8,128)} %gather_fusion.3, f32[48,128,128]{2,1,0:T(8,128)S(1)} %copy-done), kind=kOutput, calls=%fused_computation.124 | convolution fusion | flops 150994944 | bytes 3932160 | tf_op jit(solution)/shard_map/pab,prb->pra/dot_general | solution.py:44
  154.7 9.5 %all-gather.3 = f32[32,16,128]{2,1,0:T(8,128)} all-gather(f32[4,16,128]{2,1,0:T(8,128)S(1)} %copy.49), channel_id=5, replica_groups=mesh['src'=4,'delay'=8] {'delay'}, dimensions={0}, use_global_device_ids=true | all-gather | bytes 294912 | tf_op jit(solution)/shard_map/all_gather | solution.py:51
  (52 shorter events, 14.3 us)
Async XLA Ops:
  0.0 31.8 %copy-start = (f32[48,128,128]{2,1,0:T(8,128)S(1)}, f32[48,128,128]{2,1,0:T(8,128)}, u32[]{:S(2)}) copy-start(f32[48,128,128]{2,1,0:T(8,128)} %param.9) | copy-start | bytes 9437188
  2.1 46.6 %copy-start.2 = (f32[4,4,16,128]{3,2,1,0:T(8,128)S(1)}, f32[4,4,16,128]{3,2,1,0:T(8,128)}, u32[]{:S(2)}) copy-start(f32[4,4,16,128]{3,2,1,0:T(8,128)} %param.13) | copy-start | bytes 393220
  23.7 27.4 %copy-start.1 = (f32[4,128,128]{2,1,0:T(8,128)S(1)}, f32[4,128,128]{2,1,0:T(8,128)}, u32[]{:S(2)}) copy-start(f32[4,128,128]{2,1,0:T(8,128)} %param.12) | copy-start | bytes 786436
  23.7 45.0 %collective-permute-start = (f32[16,16,128]{2,1,0:T(8,128)}, f32[16,16,128]{2,1,0:T(8,128)}, u32[]{:S(2)}, u32[]{:S(2)}) collective-permute-start(f32[16,16,128]{2,1,0:T(8,128)} %dynamic-slice_bitcast_fusion.2), channel_id=1, source_target_pairs={{0,1},{1,2},{2,3},{3,4},{4,5},{5,6},{6,7},{8,9},{9,10},{10,11},{11... | collective-permute-start | bytes 393224 | tf_op jit(solution)/shard_map/ppermute | solution.py:10
  31.1 6.6 %copy-start.5 = (s32[48]{0:T(128)S(1)}, s32[48]{0:T(128)}, u32[]{:S(2)}) copy-start(s32[48]{0:T(128)} %get-tuple-element.21) | copy-start | bytes 580
  31.8 17.5 %copy-start.7 = (f32[48]{0:T(128)}, f32[48]{0:T(128)S(1)}, u32[]{:S(2)}) copy-start(f32[48]{0:T(128)S(1)} %compare_convert_fusion) | copy-start | bytes 580
  49.3 29.6 %copy-start.6 = (s32[48]{0:T(128)S(1)}, s32[48]{0:T(128)}, u32[]{:S(2)}) copy-start(s32[48]{0:T(128)} %get-tuple-element.21) | copy-start | bytes 580
  49.3 29.6 %copy-start.8 = (f32[48]{0:T(128)S(1)}, f32[48]{0:T(128)}, u32[]{:S(2)}) copy-start(f32[48]{0:T(128)} %copy-done.7) | copy-start | bytes 580
  70.3 22.6 %copy-start.4 = (f32[1,4,16,128]{3,2,1,0:T(8,128)S(1)}, f32[1,4,16,128]{3,2,1,0:T(8,128)}, u32[]{:S(2)}) copy-start(f32[1,4,16,128]{3,2,1,0:T(8,128)} %get-tuple-element.18) | copy-start | bytes 98308
  88.7 27.6 %copy-start.9 = (f32[48]{0:T(128)S(1)}, f32[48]{0:T(128)}, u32[]{:S(2)}) copy-start(f32[48]{0:T(128)} %copy-done.7) | copy-start | bytes 580
  90.6 16.4 %collective-permute-start.1 = (f32[16,16,128]{2,1,0:T(8,128)S(1)}, f32[16,16,128]{2,1,0:T(8,128)S(1)}, u32[]{:S(2)}, u32[]{:S(2)}) collective-permute-start(f32[16,16,128]{2,1,0:T(8,128)S(1)} %dynamic-slice_bitcast_fusion.1), channel_id=1, source_target_pairs={{0,1},{1,2},{2,3},{3,4},{4,5},{5,6},{6,7},{8,9},{9,10},{10,11},{11... | collective-permute-start | bytes 393224 | tf_op jit(solution)/shard_map/ppermute | solution.py:10
  107.7 23.4 %copy-start.3 = (f32[1,4,16,128]{3,2,1,0:T(8,128)S(1)}, f32[1,4,16,128]{3,2,1,0:T(8,128)}, u32[]{:S(2)}) copy-start(f32[1,4,16,128]{3,2,1,0:T(8,128)} %get-tuple-element.17) | copy-start | bytes 98308
  128.8 16.2 %collective-permute-start.2 = (f32[16,16,128]{2,1,0:T(8,128)S(1)}, f32[16,16,128]{2,1,0:T(8,128)S(1)}, u32[]{:S(2)}, u32[]{:S(2)}) collective-permute-start(f32[16,16,128]{2,1,0:T(8,128)S(1)} %dynamic-slice_bitcast_fusion), channel_id=1, source_target_pairs={{0,1},{1,2},{2,3},{3,4},{4,5},{5,6},{6,7},{8,9},{9,10},{10,11},{11... | collective-permute-start | bytes 393224 | tf_op jit(solution)/shard_map/ppermute | solution.py:10
